TPU v7x, 32 devices: a whole 2x2x4 slice. The times are simulated.
32 devices in a mesh: row: 8 (over y, x, core), col: 4 (over z).
Axes of the slice: x: 2, y: 2, z: 4, core: 2. Of those that a mesh axis runs over, the one named last changes fastest.
Arguments:
- classes: int32 [128, 64], P('row', 'col'), may hold values from 0 to 15
- features: bfloat16 [128, 64, 128], P('row', 'col'), may hold values from -6 to 6
- cotangent: bfloat16 [128, 64, 128], P('row', 'col'), may hold values from -6 to 6
- table: float32 [16, 128], replicated, may hold values from -6 to 6
- norm_gain: float32 [128], replicated, may hold values from 0.5 to 1.5
- in_weight: bfloat16 [128, 512], replicated, may hold values from -0.5 to 0.5
- scan_weight: bfloat16 [256, 160], replicated, may hold values from -0.375 to 0.375
- step_weight: float32 [4, 8, 256], replicated, may hold values from -2 to 2
- step_bias: float32 [4, 256], replicated, may hold values from -6 to -2.5
- decay_log: float32 [4, 16, 256], replicated, may hold values from -4 to 2
- skip_gain: float32 [4, 256], replicated, may hold values from 0.5 to 1.5
- output_gain: float32 [256], replicated, may hold values from 0.5 to 1.5
- output_weight: bfloat16 [256, 128], replicated, may hold values from -0.375 to 0.375
Outputs:
- feature_grad: bfloat16 [128, 64, 128], P('row', 'col')
- in_weight_grad: float32 [128, 512], replicated
- scan_weight_grad: float32 [256, 160], replicated
- step_weight_grad: float32 [4, 8, 256], replicated
- step_bias_grad: float32 [4, 256], replicated
- decay_log_grad: float32 [4, 16, 256], replicated
- skip_gain_grad: float32 [4, 256], replicated
- norm_gain_grad: float32 [128], replicated
- output_gain_grad: float32 [256], replicated
- output_weight_grad: float32 [256, 128], replicated
All inputs are finite; a program needn't handle non-finite values.
Results may differ from a plain program's by a relative error of at most 0.0076.
Values sent between devices are 32-bit elements; how exact they have to be, the bound alone decides.
A program may use at most 320 MiB of HBM per device.

v0:
```python
import functools
import math

import jax
import jax.numpy as jnp
from jax import lax
from jax.experimental import pallas as pl
from jax.experimental.pallas import tpu as pltpu
from jax.sharding import PartitionSpec as P

EPS = 1e-05
HIGHEST = lax.Precision.HIGHEST
MESH = pl.DeviceIdType.MESH
LANES = 128
SUB = 8
LOG2E = math.log2(math.e)
VMEM = pl.BlockSpec(memory_space=pltpu.VMEM)
BIG = 60 * 1024 * 1024


def layer_norm(rows, gain):
    average = jnp.mean(rows, axis=-1, keepdims=True)
    centred = rows - average
    spread = jnp.mean(centred * centred, axis=-1, keepdims=True)
    return centred * lax.rsqrt(spread + EPS) * gain


def silu_slope(before):
    sigma = jax.nn.sigmoid(before)
    return sigma * (1.0 + before * (1.0 - sigma))


def embed(features, classes, table):
    labels = jnp.arange(table.shape[0], dtype=jnp.int32)
    onehot = (classes[..., None] == labels).astype(jnp.float32)
    lookup = jnp.einsum("hwk,kd->hwd", onehot, table, precision=HIGHEST)
    return features.astype(jnp.float32) + lookup


def gate_output(total, gate_in, output_gain):
    return layer_norm(total, output_gain) * jax.nn.silu(gate_in)


def greet(axes):
    barrier = pltpu.get_barrier_semaphore()
    partners = 0
    for axis in axes:
        count = lax.axis_size(axis)
        me = lax.axis_index(axis)
        for d in range(1, count):
            pl.semaphore_signal(
                barrier, inc=1, device_id={axis: lax.rem(me + d, count)}, device_id_type=MESH
            )
            partners += 1
    pl.semaphore_wait(barrier, partners)


def exchange_kernel(axes, *refs):
    k = len(axes)
    sources, results, sems = refs[:k], refs[k : 2 * k], refs[2 * k :]
    greet(axes)
    copies = []
    for i, axis in enumerate(axes):
        count = lax.axis_size(axis)
        me = lax.axis_index(axis)
        for d in range(1, count):
            target = lax.rem(me + d, count)
            copy = pltpu.make_async_remote_copy(
                src_ref=sources[i].at[target],
                dst_ref=results[i].at[me],
                send_sem=sems[2 * i].at[d],
                recv_sem=sems[2 * i + 1].at[d],
                device_id={axis: target},
                device_id_type=MESH,
            )
            copy.start()
            copies.append(copy)
    for i, axis in enumerate(axes):
        me = lax.axis_index(axis)
        results[i][me] = sources[i][me]
    for copy in copies:
        copy.wait()


def exchange(arrays, axes, ident):
    scratch = []
    for axis in axes:
        count = lax.axis_size(axis)
        scratch += [pltpu.SemaphoreType.DMA((count,)), pltpu.SemaphoreType.DMA((count,))]
    return pl.pallas_call(
        functools.partial(exchange_kernel, axes),
        out_shape=[jax.ShapeDtypeStruct(a.shape, a.dtype) for a in arrays],
        in_specs=[VMEM] * len(arrays),
        out_specs=[VMEM] * len(arrays),
        scratch_shapes=scratch,
        compiler_params=pltpu.CompilerParams(collective_id=ident, has_side_effects=True),
    )(*arrays)


def reduce_kernel(x_ref, out_ref, first, partial, second, sems):
    rows, cols = lax.axis_size("row"), lax.axis_size("col")
    r, c = lax.axis_index("row"), lax.axis_index("col")
    greet(("row", "col"))

    def spread(axis, source, result, phase):
        count = lax.axis_size(axis)
        me = lax.axis_index(axis)
        copies = []
        for d in range(1, count):
            target = lax.rem(me + d, count)
            copy = pltpu.make_async_remote_copy(
                src_ref=source(target),
                dst_ref=result(me, d),
                send_sem=sems.at[phase, 0, d],
                recv_sem=sems.at[phase, 1, d],
                device_id={axis: target},
                device_id_type=MESH,
            )
            copy.start()
            copies.append(copy)
        for copy in copies:
            copy.wait()

    spread("row", lambda t: x_ref.at[t], lambda me, d: first.at[d - 1], 0)
    acc = x_ref[r]
    for d in range(rows - 1):
        acc = acc + first[d]
    partial[...] = acc
    spread("col", lambda t: partial.at[t], lambda me, d: second.at[d - 1], 1)
    acc = partial[c]
    for d in range(cols - 1):
        acc = acc + second[d]
    out_ref[r, c] = acc
    spread("col", lambda t: out_ref.at[r, c], lambda me, d: out_ref.at[r, me], 2)
    spread("row", lambda t: out_ref.at[r], lambda me, d: out_ref.at[me], 3)


def reduce_all(flat, ident):
    rows, cols = lax.axis_size("row"), lax.axis_size("col")
    part = flat.shape[2:]
    most = max(rows, cols)
    return pl.pallas_call(
        reduce_kernel,
        out_shape=jax.ShapeDtypeStruct(flat.shape, flat.dtype),
        in_specs=[VMEM],
        out_specs=VMEM,
        scratch_shapes=[
            pltpu.VMEM((rows - 1, cols) + part, jnp.float32),
            pltpu.VMEM((cols,) + part, jnp.float32),
            pltpu.VMEM((cols - 1,) + part, jnp.float32),
            pltpu.SemaphoreType.DMA((4, 2, most)),
        ],
        compiler_params=pltpu.CompilerParams(collective_id=ident, has_side_effects=True),
    )(flat)


def half(ref, k, h, t):
    return ref[k, h, pl.ds(t, 1), :]


def fill_lines(v_ref, s_ref, p_ref, wide, sv, steps):
    count = v_ref.shape[0]
    states = wide.shape[2] // count
    for k in range(2):
        for which in range(2):
            for n in range(states):
                col = (2 * k + which) * states + n
                wide[k, which, pl.ds(n, count, stride=states), :] = jnp.broadcast_to(
                    p_ref[:, col : col + 1], (count, LANES)
                )
        for h in range(sv.shape[1]):
            cols = slice(h * LANES, (h + 1) * LANES)
            step = s_ref[k][:, cols]
            steps[k, h] = step
            sv[k, h] = step * v_ref[:, cols]


def walk(lines, tile, blocks, group, start, step):
    def outer(b, carry):
        def inner(j, carry):
            rising = b * (tile * lines) + j
            falling = (blocks - 1 - b) * (tile * lines) + (tile - 1 - j)
            tokens = [[base + line * tile for line in group] for base in (rising, falling)]
            return step(carry, tokens)

        return lax.fori_loop(0, tile, inner, carry, unroll=2)

    return lax.fori_loop(0, blocks, outer, start)


def groups_of(lines):
    size = 2 if lines % 2 == 0 else 1
    return [tuple(range(g, g + size)) for g in range(0, lines, size)]


def fold(ref, k, h, count):
    total = ref[k, h, pl.ds(0, count, stride=SUB), :]
    for s in range(1, SUB):
        total = total + ref[k, h, pl.ds(s, count, stride=SUB), :]
    return total


def forward_kernel(lines, tile, v_ref, s_ref, p_ref, rate_ref, skip_ref, y_ref, wide, sv, steps, out8):
    count = v_ref.shape[0]
    blocks = count // (lines * tile)
    states = wide.shape[2] // count
    eh, nh = sv.shape[1], states // SUB
    fill_lines(v_ref, s_ref, p_ref, wide, sv, steps)
    for group in groups_of(lines):

        def step(carry, tokens, group=group):
            new = []
            i = 0
            for k in range(2):
                for t in tokens[k]:
                    drive = [half(sv, k, h, t) for h in range(eh)]
                    pace = [half(steps, k, h, t) for h in range(eh)]
                    sums = [None] * eh
                    for m in range(nh):
                        at = pl.ds(pl.multiple_of(t * states + m * SUB, SUB), SUB)
                        source = wide[k, 0, at, :]
                        probe = wide[k, 1, at, :]
                        for h in range(eh):
                            rate = rate_ref[k, m * SUB : (m + 1) * SUB, h * LANES : (h + 1) * LANES]
                            state = jnp.exp2(pace[h] * rate) * carry[i] + source * drive[h]
                            i += 1
                            new.append(state)
                            term = probe * state
                            sums[h] = term if sums[h] is None else sums[h] + term
                    for h in range(eh):
                        out8[k, h, pl.ds(pl.multiple_of(t * SUB, SUB), SUB), :] = sums[h]
            return tuple(new)

        zero = jnp.zeros((SUB, LANES), jnp.float32)
        walk(lines, tile, blocks, group, (zero,) * (2 * len(group) * eh * nh), step)
    for h in range(eh):
        cols = slice(h * LANES, (h + 1) * LANES)
        skip = skip_ref[0:1, cols] + skip_ref[1:2, cols]
        y_ref[:, cols] = fold(out8, 0, h, count) + fold(out8, 1, h, count) + skip * v_ref[:, cols]


def backward_kernel(
    lines, tile, v_ref, s_ref, p_ref, rate_ref, skip_ref, g_ref,
    dv_ref, ds_ref, dp_ref, dr_ref,
    wide, sv, steps, up, before, decay, drive8, pace8,
):
    count = v_ref.shape[0]
    blocks = count // (lines * tile)
    states = wide.shape[2] // count
    eh, nh = sv.shape[1], states // SUB
    fill_lines(v_ref, s_ref, p_ref, wide, sv, steps)
    for h in range(eh):
        up[0, h] = g_ref[:, h * LANES : (h + 1) * LANES]
    zero = jnp.zeros((SUB, LANES), jnp.float32)

    def rate_of(k, m, h):
        return rate_ref[k, m * SUB : (m + 1) * SUB, h * LANES : (h + 1) * LANES]

    dr_ref[...] = jnp.zeros_like(dr_ref)
    for group in groups_of(lines):

        def advance(carry, tokens):
            new = []
            i = 0
            for k in range(2):
                for t in tokens[k]:
                    drive = [half(sv, k, h, t) for h in range(eh)]
                    pace = [half(steps, k, h, t) for h in range(eh)]
                    g = [half(up, 0, h, t) for h in range(eh)]
                    for m in range(nh):
                        at = pl.ds(pl.multiple_of(t * states + m * SUB, SUB), SUB)
                        source = wide[k, 0, at, :]
                        total = None
                        for h in range(eh):
                            a = jnp.exp2(pace[h] * rate_of(k, m, h))
                            before[k, h, at, :] = carry[i]
                            decay[k, h, at, :] = a
                            state = a * carry[i] + source * drive[h]
                            i += 1
                            new.append(state)
                            term = g[h] * state
                            total = term if total is None else total + term
                        wide[k, 2, at, :] = total
            return tuple(new)

        def retreat(carry, tokens):
            grads, rates = carry
            rates = list(rates)
            new = []
            i = 0
            for k in range(2):
                for t in tokens[1 - k]:
                    drive = [half(sv, k, h, t) for h in range(eh)]
                    pace = [half(steps, k, h, t) for h in range(eh)]
                    g = [half(up, 0, h, t) for h in range(eh)]
                    dd = [None] * eh
                    dp = [None] * eh
                    for m in range(nh):
                        at = pl.ds(pl.multiple_of(t * states + m * SUB, SUB), SUB)
                        source = wide[k, 0, at, :]
                        probe = wide[k, 1, at, :]
                        total = None
                        for h in range(eh):
                            grad = grads[i] + probe * g[h]
                            i += 1
                            term = grad * drive[h]
                            total = term if total is None else total + term
                            term = grad * source
                            dd[h] = term if dd[h] is None else dd[h] + term
                            carried = decay[k, h, at, :] * grad
                            q = carried * before[k, h, at, :]
                            term = q * rate_of(k, m, h)
                            dp[h] = term if dp[h] is None else dp[h] + term
                            j = (k * nh + m) * eh + h
                            rates[j] = rates[j] + q * pace[h]
                            new.append(carried)
                        wide[k, 3, at, :] = total
                    for h in range(eh):
                        at8 = pl.ds(pl.multiple_of(t * SUB, SUB), SUB)
                        drive8[k, h, at8, :] = dd[h]
                        pace8[k, h, at8, :] = dp[h]
            return (tuple(new), tuple(rates))

        chains = 2 * len(group) * eh * nh
        walk(lines, tile, blocks, group, (zero,) * chains, advance)
        unused, rates = walk(
            lines, tile, blocks, group, ((zero,) * chains, (zero,) * (2 * eh * nh)), retreat
        )
        for k in range(2):
            for m in range(nh):
                for h in range(eh):
                    dr_ref[k, m * SUB : (m + 1) * SUB, h * LANES : (h + 1) * LANES] += rates[
                        (k * nh + m) * eh + h
                    ]
    for h in range(eh):
        cols = slice(h * LANES, (h + 1) * LANES)
        value = v_ref[:, cols]
        dv = (skip_ref[0:1, cols] + skip_ref[1:2, cols]) * g_ref[:, cols]
        for k in range(2):
            drive = fold(drive8, k, h, count)
            dv = dv + drive * steps[k, h]
            ds_ref[k, :, cols] = drive * value + fold(pace8, k, h, count) * (1.0 / LOG2E)
        dv_ref[:, cols] = dv
    for k in range(2):
        for which in range(2):
            for n in range(states):
                col = (2 * k + which) * states + n
                dp_ref[:, col : col + 1] = jnp.sum(
                    wide[k, 3 - which, pl.ds(n, count, stride=states), :], axis=-1, keepdims=True
                )


def scan_scratch(count, states, inner, slots):
    eh = inner // LANES
    return [
        pltpu.VMEM((2, slots, count * states, LANES), jnp.float32),
        pltpu.VMEM((2, eh, count, LANES), jnp.float32),
        pltpu.VMEM((2, eh, count, LANES), jnp.float32),
    ]


def scan_forward(lines, tile, values, steps, flows, rate, skip):
    count, inner = values.shape
    states = rate.shape[1]
    eh = inner // LANES
    return pl.pallas_call(
        functools.partial(forward_kernel, lines, tile),
        out_shape=jax.ShapeDtypeStruct((count, inner), jnp.float32),
        in_specs=[VMEM] * 5,
        out_specs=VMEM,
        scratch_shapes=scan_scratch(count, states, inner, 2)
        + [pltpu.VMEM((2, eh, count * SUB, LANES), jnp.float32)],
        compiler_params=pltpu.CompilerParams(vmem_limit_bytes=BIG),
    )(values, steps, flows, rate, skip)


def scan_backward(lines, tile, values, steps, flows, rate, skip, upstream):
    count, inner = values.shape
    states = rate.shape[1]
    eh = inner // LANES
    return pl.pallas_call(
        functools.partial(backward_kernel, lines, tile),
        out_shape=[
            jax.ShapeDtypeStruct((count, inner), jnp.float32),
            jax.ShapeDtypeStruct((2, count, inner), jnp.float32),
            jax.ShapeDtypeStruct((count, 4 * states), jnp.float32),
            jax.ShapeDtypeStruct((2, states, inner), jnp.float32),
        ],
        in_specs=[VMEM] * 6,
        out_specs=[VMEM] * 4,
        scratch_shapes=scan_scratch(count, states, inner, 4)
        + [
            pltpu.VMEM((1, eh, count, LANES), jnp.float32),
            pltpu.VMEM((2, eh, count * states, LANES), jnp.float32),
            pltpu.VMEM((2, eh, count * states, LANES), jnp.float32),
            pltpu.VMEM((2, eh, count * SUB, LANES), jnp.float32),
            pltpu.VMEM((2, eh, count * SUB, LANES), jnp.float32),
        ],
        compiler_params=pltpu.CompilerParams(vmem_limit_bytes=BIG),
    )(values, steps, flows, rate, skip, upstream)


def local(
    classes, features, cotangent, table, norm_gain, in_weight, scan_weight, step_weight,
    step_bias, decay_log, skip_gain, output_gain, output_weight,
):
    tile_rows, tile_cols, model_width = features.shape
    inner = output_weight.shape[0]
    count = tile_rows * tile_cols
    rows, cols = lax.axis_size("row"), lax.axis_size("col")
    rank = step_weight.shape[1]
    states = decay_log.shape[1]
    group = rank + 2 * states
    grad_scale = float(count * rows * cols) ** (-0.5)
    row_lines, col_lines = tile_rows // cols, tile_cols // rows
    rate = -jnp.exp(decay_log)
    rate2 = rate * LOG2E

    def to_lines(x, ident):
        along = x.reshape(cols, row_lines * tile_cols, x.shape[-1])
        down = jnp.swapaxes(x.reshape(tile_rows, tile_cols, x.shape[-1]), 0, 1)
        down = down.reshape(rows, col_lines * tile_rows, x.shape[-1])
        a, d = exchange((along, down), ("col", "row"), ident)
        return (a.reshape(count, x.shape[-1]), d.reshape(count, x.shape[-1]))

    def from_lines(a, d, ident):
        a, d = exchange(
            (a.reshape(cols, -1, a.shape[-1]), d.reshape(rows, -1, d.shape[-1])), ("col", "row"), ident
        )
        d = jnp.swapaxes(d.reshape(tile_cols, tile_rows, d.shape[-1]), 0, 1)
        return a.reshape(count, -1) + d.reshape(count, -1)

    embedded = embed(features, classes, table).reshape(count, model_width)
    normed = layer_norm(embedded, norm_gain).astype(jnp.bfloat16)
    mixed = jnp.dot(normed, in_weight, preferred_element_type=jnp.float32)
    values = jax.nn.silu(mixed[:, :inner]).astype(jnp.bfloat16)
    gate_in = mixed[:, inner:]
    line_values = to_lines(values.astype(jnp.float32), 1)

    prepared = []
    outputs = []
    for pair in range(2):
        v = line_values[pair]
        dirs = (2 * pair, 2 * pair + 1)
        weight = scan_weight[:, dirs[0] * group : (dirs[1] + 1) * group]
        vb = v.astype(jnp.bfloat16)
        projected = jnp.dot(vb, weight, preferred_element_type=jnp.float32)
        lowrank = [projected[:, i * group : i * group + rank] for i in range(2)]
        before = jnp.stack(
            [
                jnp.dot(lowrank[i], step_weight[dirs[i]], precision=HIGHEST) + step_bias[dirs[i]]
                for i in range(2)
            ]
        )
        steps = jax.nn.softplus(before)
        flows = jnp.concatenate(
            [projected[:, i * group + rank : (i + 1) * group] for i in range(2)], axis=1
        )
        lines, tile = ((row_lines, tile_cols), (col_lines, tile_rows))[pair]
        args = (lines, tile, v, steps, flows, rate2[dirs[0] : dirs[1] + 1], skip_gain[dirs[0] : dirs[1] + 1])
        outputs.append(scan_forward(*args))
        prepared.append((args, vb, weight, lowrank, before))
    total = from_lines(outputs[0], outputs[1], 2)

    gated = gate_output(total, gate_in, output_gain).astype(jnp.bfloat16)
    upstream = cotangent.reshape(count, model_width)
    output_weight_grad = jnp.dot(gated.T, upstream, preferred_element_type=jnp.float32)
    d_gated = jnp.dot(upstream, output_weight.T, preferred_element_type=jnp.float32)
    unused, gate_pull = jax.vjp(gate_output, total, gate_in, output_gain)
    d_total, d_gate_in, output_gain_grad = gate_pull(d_gated)
    line_grads = to_lines(d_total, 3)

    d_lines, scan_grads, stepw_grads, stepb_grads, decay_grads, skip_grads = ([], [], [], [], [], [])
    for pair in range(2):
        args, vb, weight, lowrank, before = prepared[pair]
        g = line_grads[pair]
        dv, ds, dflow, drate = scan_backward(*args, g)
        d_before = ds * jax.nn.sigmoid(before)
        parts = []
        for i in range(2):
            k = 2 * pair + i
            parts.append(jnp.dot(d_before[i], step_weight[k].T, precision=HIGHEST))
            parts.append(dflow[:, i * 2 * states : (i + 1) * 2 * states])
            stepw_grads.append(jnp.dot(lowrank[i].T, d_before[i], precision=HIGHEST))
            stepb_grads.append(jnp.sum(d_before[i], axis=0))
            skip_grads.append(jnp.sum(g * args[2], axis=0))
        decay_grads.append(drate * rate[2 * pair : 2 * pair + 2])
        d_projected = jnp.concatenate(parts, axis=1).astype(jnp.bfloat16)
        scan_grads.append(jnp.dot(vb.T, d_projected, preferred_element_type=jnp.float32))
        d_lines.append(jnp.dot(d_projected, weight.T, preferred_element_type=jnp.float32) + dv)
    d_values = from_lines(d_lines[0], d_lines[1], 4)

    d_mixed = jnp.concatenate([d_values * silu_slope(mixed[:, :inner]), d_gate_in], axis=1).astype(
        jnp.bfloat16
    )
    in_weight_grad = jnp.dot(normed.T, d_mixed, preferred_element_type=jnp.float32)
    d_normed = jnp.dot(d_mixed, in_weight.T, preferred_element_type=jnp.float32)
    unused, norm_pull = jax.vjp(layer_norm, embedded, norm_gain)
    d_embedded, norm_gain_grad = norm_pull(d_normed)
    feature_grad = (
        (upstream.astype(jnp.float32) + d_embedded)
        .astype(jnp.bfloat16)
        .reshape(tile_rows, tile_cols, model_width)
    )
    grads = (
        in_weight_grad,
        jnp.concatenate(scan_grads, axis=1),
        jnp.stack(stepw_grads),
        jnp.stack(stepb_grads),
        jnp.concatenate(decay_grads, axis=0),
        jnp.stack(skip_grads),
        norm_gain_grad,
        output_gain_grad,
        output_weight_grad,
    )
    flat = jnp.concatenate([g.reshape(-1, LANES) for g in grads], axis=0)
    used = flat.shape[0]
    unit = rows * cols * SUB
    padded = -(-used // unit) * unit
    flat = jnp.pad(flat, ((0, padded - used), (0, 0))).reshape(rows, cols, padded // (rows * cols), LANES)
    flat = reduce_all(flat, 5).reshape(padded, LANES) * grad_scale
    summed = []
    place = 0
    for g in grads:
        length = g.size // LANES
        summed.append(flat[place : place + length].reshape(g.shape))
        place += length
    return (feature_grad, *summed)


def solution(mesh):
    in_specs = (P("row", "col"), P("row", "col", None), P("row", "col", None)) + (P(),) * 10
    out_specs = (P("row", "col", None),) + (P(),) * 9
    return jax.shard_map(local, mesh=mesh, in_specs=in_specs, out_specs=out_specs, check_vma=False)
```

profile of v0, /device:TPU:1, one launch (start us, length us, event | category | flops | bytes accessed | tf_op | source)
XLA Modules:
  0.0 184.6 jit_solution(12031956220874727906)
XLA Ops:
  0.7 1.2 fusion.89
  3.9 0.9 copy.51
  4.7 11.7 %shard_map.204 = (f32[4,64,256]{2,1,0:T(8,128)}, f32[8,32,256]{2,1,0:T(8,128)}) custom-call(f32[4,64,256]{2,1,0:T(8,128)} %bitcast.174, f32[8,32,256]{2,1,0:T(8,128)} %bitcast.181), custom_call_target="tpu_custom_call" | custom-call | tf_op jit(solution)/shard_map/pallas_call | solution.py:90
  16.5 1.1 fusion.40
  18.6 1.1 compare_select_fusion.1.s_ref
  19.9 0.8 pad_maximum_fusion.6.p_ref
  20.7 0.6 exponential_negate_fusion
  21.3 0.6 fusion.86
  22.6 8.5 %shard_map.205 = f32[256,256]{1,0:T(8,128)} custom-call(f32[256,256]{1,0:T(8,128)} %bitcast.153, f32[2,256,256]{2,1,0:T(8,128)} %compare_select_fusion.1.s_ref, f32[256,64]{1,0:T(8,128)} %pad_maximum_fusion.6.p_ref, f32[2,16,256]{2,1,0:T(8,128)} %get-tuple-element.92.rate_ref, f32[2,256]{1,0:T(2,128)} %get-tuple-element.94.skip_ref), custom_call_target="tpu_custom_call" | custom-call | tf_op jit(solution)/shard_map/pallas_call | solution.py:366
  32.2 1.1 compare_select_fusion.s_ref
  33.5 0.8 pad_maximum_fusion.7.p_ref
  34.3 8.3 %shard_map.206 = f32[256,256]{1,0:T(8,128)} custom-call(f32[256,256]{1,0:T(8,128)} %bitcast.156, f32[2,256,256]{2,1,0:T(8,128)} %compare_select_fusion.s_ref, f32[256,64]{1,0:T(8,128)} %pad_maximum_fusion.7.p_ref, f32[2,16,256]{2,1,0:T(8,128)} %get-tuple-element.91.rate_ref, f32[2,256]{1,0:T(2,128)} %get-tuple-element.93.skip_ref), custom_call_target="tpu_custom_call" | custom-call | tf_op jit(solution)/shard_map/pallas_call | solution.py:366
  42.6 10.7 %shard_map.207 = (f32[4,64,256]{2,1,0:T(8,128)}, f32[8,32,256]{2,1,0:T(8,128)}) custom-call(f32[4,64,256]{2,1,0:T(8,128)} %bitcast.177, f32[8,32,256]{2,1,0:T(8,128)} %bitcast.178), custom_call_target="tpu_custom_call" | custom-call | tf_op jit(solution)/shard_map/pallas_call | solution.py:90
  53.4 1.1 copy.56
  54.7 0.6 div.67
  55.4 0.6 copy-done.27
  56.0 1.5 multiply_reduce_fusion.3
  58.4 0.7 multiply_reduce_fusion
  59.3 0.9 copy.58
  60.2 11.1 %shard_map.208 = (f32[4,64,256]{2,1,0:T(8,128)}, f32[8,32,256]{2,1,0:T(8,128)}) custom-call(f32[4,64,256]{2,1,0:T(8,128)} %bitcast.172, f32[8,32,256]{2,1,0:T(8,128)} %bitcast.182), custom_call_target="tpu_custom_call" | custom-call | tf_op jit(solution)/shard_map/pallas_call | solution.py:90
  71.4 18.4 %shard_map.209 = (f32[256,256]{1,0:T(8,128)}, f32[2,256,256]{2,1,0:T(8,128)}, f32[256,64]{1,0:T(8,128)}, f32[2,16,256]{2,1,0:T(8,128)}) custom-call(f32[256,256]{1,0:T(8,128)} %bitcast.154, f32[2,256,256]{2,1,0:T(8,128)} %compare_select_fusion.1.s_ref, f32[256,64]{1,0:T(8,128)} %pad_maximum_fusion.6.p_ref, f32[2,16,256]{2,1,0:T(8,128)} %get-tuple-element.92.rate_ref, ...), custom_call_target="tpu_custom_call" | custom-call | tf_op jit(solution)/shard_map/pallas_call | solution.py:381
  89.7 0.9 convert.31
  90.6 0.7 fusion.85
  91.3 1.2 divide_multiply_fusion.1
  94.8 0.9 convolution_add_fusion.5
  95.6 18.4 %shard_map.210 = (f32[256,256]{1,0:T(8,128)}, f32[2,256,256]{2,1,0:T(8,128)}, f32[256,64]{1,0:T(8,128)}, f32[2,16,256]{2,1,0:T(8,128)}) custom-call(f32[256,256]{1,0:T(8,128)} %bitcast.157, f32[2,256,256]{2,1,0:T(8,128)} %compare_select_fusion.s_ref, f32[256,64]{1,0:T(8,128)} %pad_maximum_fusion.7.p_ref, f32[2,16,256]{2,1,0:T(8,128)} %get-tuple-element.91.rate_ref, ...), custom_call_target="tpu_custom_call" | custom-call | tf_op jit(solution)/shard_map/pallas_call | solution.py:381
  114.0 0.9 convert.34
  114.9 0.7 fusion.84
  115.7 1.2 divide_multiply_fusion
  118.6 0.9 convolution_add_fusion.4
  119.5 10.7 %shard_map.211 = (f32[4,64,256]{2,1,0:T(8,128)}, f32[8,32,256]{2,1,0:T(8,128)}) custom-call(f32[4,64,256]{2,1,0:T(8,128)} %bitcast.179, f32[8,32,256]{2,1,0:T(8,128)} %bitcast.180), custom_call_target="tpu_custom_call" | custom-call | tf_op jit(solution)/shard_map/pallas_call | solution.py:90
  130.2 1.1 copy.63
  131.6 0.6 copy-done.35
  132.5 0.7 copy-done.29
  134.1 0.7 add_convert_fusion
  135.0 0.9 copy-done.3
  136.2 0.7 copy-done.1
  138.6 0.7 copy-done.11
  139.6 0.9 copy-done.7
  140.6 0.8 copy-done.16
  142.4 1.0 pad.4
  143.4 34.0 %shard_map.212 = f32[8,4,48,128]{3,2,1,0:T(8,128)} custom-call(f32[8,4,48,128]{3,2,1,0:T(8,128)} %bitcast.162), custom_call_target="tpu_custom_call" | custom-call | tf_op jit(solution)/shard_map/pallas_call | solution.py:142
  177.4 1.2 broadcast_multiply_fusion
  178.7 0.7 reshape.276
  179.6 0.8 copy.65
  180.4 0.6 reshape.278
  181.6 0.6 reshape.280
  183.9 0.7 slice.219
  (145 shorter events, 17.6 us)
Async XLA Ops:
  0.6 2.9 %copy-start = (bf16[128,512]{1,0:T(8,128)(2,1)S(1)}, bf16[128,512]{1,0:T(8,128)(2,1)}, u32[]{:S(2)}) copy-start(bf16[128,512]{1,0:T(8,128)(2,1)} %param.18) | copy-start | bytes 393220
  2.2 0.6 copy-start.28
  2.8 0.7 copy-start.34
  3.9 0.9 copy-start.5
  4.7 11.8 %copy-start.31 = (f32[4,256]{1,0:T(4,128)S(1)}, f32[4,256]{1,0:T(4,128)}, u32[]{:S(2)}) copy-start(f32[4,256]{1,0:T(4,128)} %param.21) | copy-start | bytes 12292
  4.7 11.8 %copy-start.9 = (bf16[256,160]{0,1:T(8,128)(2,1)S(1)}, bf16[256,160]{0,1:T(8,128)(2,1)}, u32[]{:S(2)}) copy-start(bf16[256,160]{0,1:T(8,128)(2,1)} %param.19) | copy-start | bytes 245764
  16.5 1.2 copy-start.22
  19.9 0.8 copy-start.23
  21.3 0.7 copy-start.32
  22.6 8.5 %copy-start.2 = (f32[8,32,256]{2,1,0:T(8,128)S(1)}, f32[8,32,256]{2,1,0:T(8,128)}, u32[]{:S(2)}) copy-start(f32[8,32,256]{2,1,0:T(8,128)} %get-tuple-element.27) | copy-start | bytes 786436
  53.3 1.2 copy-start.6
  54.5 0.8 copy-start.14
  54.5 0.9 copy-start.24
  55.3 0.7 copy-start.27
  57.7 0.7 copy-start.30
  59.3 0.9 copy-start.4
  93.0 0.8 copy-start.17
  93.0 0.9 copy-start.18
  93.3 1.0 copy-start.12
  93.9 0.9 copy-start.10
  117.3 0.8 copy-start.19
  117.3 0.9 copy-start.20
  117.6 1.0 copy-start.13
  130.1 1.2 copy-start.21
  131.6 0.7 copy-start.35
  132.5 0.7 copy-start.29
  133.2 0.8 copy-start.15
  135.0 1.0 copy-start.3
  135.9 0.9 copy-start.1
  138.5 0.8 copy-start.11
  138.5 0.8 copy-start.25
  138.5 0.8 copy-start.26
  138.6 1.0 copy-start.8
  139.5 0.9 copy-start.7
  140.5 0.8 copy-start.16
  141.3 0.7 copy-start.33
where the time goes:
time: 186 us; the launch traced here: 185 us
  Pallas kernels  132 us (71%)
  local copies, waits for them, and re-layouts  27.4 us (15%)
  other arithmetic  13.1 us (7%)
  matrix products  10.9 us (6%)
    pallas_call x4, Pallas kernels, exchange(): pl.pallas_call(functools.partial(exchange_kernel, axes), out_shape=[jax.S...  44.3 us
    pallas_call x2, Pallas kernels, scan_backward(): pl.pallas_call(functools.partial(backward_kernel, lines, tile), out_shape...  36.7 us
    pallas_call x1, Pallas kernels, reduce_all(): pl.pallas_call(reduce_kernel, out_shape=jax.ShapeDtypeStruct(flat.shape,...  34 us
    pallas_call x2, Pallas kernels, scan_forward(): pl.pallas_call(functools.partial(forward_kernel, lines, tile), out_shape=...  16.9 us
    unnamed x77, local copies, waits for them, and re-layouts  12.2 us
    reshape x8, local copies, waits for them, and re-layouts, local(): summed.append(flat[place:place + length].reshape(g.shape))  4.43 us

commit v1 on v0

v1 whole, which is shorter than its diff:
```python
import functools
import math

import jax
import jax.numpy as jnp
from jax import lax
from jax.experimental import pallas as pl
from jax.experimental.pallas import tpu as pltpu
from jax.sharding import PartitionSpec as P

EPS = 1e-05
HIGHEST = lax.Precision.HIGHEST
MESH = pl.DeviceIdType.MESH
LANES = 128
SUB = 8
LOG2E = math.log2(math.e)
VMEM = pl.BlockSpec(memory_space=pltpu.VMEM)
BIG = 60 * 1024 * 1024


def layer_norm(rows, gain):
    average = jnp.mean(rows, axis=-1, keepdims=True)
    centred = rows - average
    spread = jnp.mean(centred * centred, axis=-1, keepdims=True)
    return centred * lax.rsqrt(spread + EPS) * gain


def silu_slope(before):
    sigma = jax.nn.sigmoid(before)
    return sigma * (1.0 + before * (1.0 - sigma))


def embed(features, classes, table):
    labels = jnp.arange(table.shape[0], dtype=jnp.int32)
    onehot = (classes[..., None] == labels).astype(jnp.float32)
    lookup = jnp.einsum("hwk,kd->hwd", onehot, table, precision=HIGHEST)
    return features.astype(jnp.float32) + lookup


def gate_output(total, gate_in, output_gain):
    return layer_norm(total, output_gain) * jax.nn.silu(gate_in)


def greet(axes):
    barrier = pltpu.get_barrier_semaphore()
    partners = 0
    for axis in axes:
        count = lax.axis_size(axis)
        me = lax.axis_index(axis)
        for d in range(1, count):
            pl.semaphore_signal(
                barrier, inc=1, device_id={axis: lax.rem(me + d, count)}, device_id_type=MESH
            )
            partners += 1
    pl.semaphore_wait(barrier, partners)


def reduce_kernel(x_ref, out_ref, first, partial, second, sems):
    rows, cols = lax.axis_size("row"), lax.axis_size("col")
    r, c = lax.axis_index("row"), lax.axis_index("col")
    greet(("row", "col"))

    def spread(axis, source, result, phase):
        count = lax.axis_size(axis)
        me = lax.axis_index(axis)
        copies = []
        for d in range(1, count):
            target = lax.rem(me + d, count)
            copy = pltpu.make_async_remote_copy(
                src_ref=source(target),
                dst_ref=result(me, d),
                send_sem=sems.at[phase, 0, d],
                recv_sem=sems.at[phase, 1, d],
                device_id={axis: target},
                device_id_type=MESH,
            )
            copy.start()
            copies.append(copy)
        for copy in copies:
            copy.wait()

    spread("row", lambda t: x_ref.at[t], lambda me, d: first.at[d - 1], 0)
    acc = x_ref[r]
    for d in range(rows - 1):
        acc = acc + first[d]
    partial[...] = acc
    spread("col", lambda t: partial.at[t], lambda me, d: second.at[d - 1], 1)
    acc = partial[c]
    for d in range(cols - 1):
        acc = acc + second[d]
    out_ref[r, c] = acc
    spread("col", lambda t: out_ref.at[r, c], lambda me, d: out_ref.at[r, me], 2)
    spread("row", lambda t: out_ref.at[r], lambda me, d: out_ref.at[me], 3)


def reduce_all(flat, ident):
    rows, cols = lax.axis_size("row"), lax.axis_size("col")
    part = flat.shape[2:]
    most = max(rows, cols)
    return pl.pallas_call(
        reduce_kernel,
        out_shape=jax.ShapeDtypeStruct(flat.shape, flat.dtype),
        in_specs=[VMEM],
        out_specs=VMEM,
        scratch_shapes=[
            pltpu.VMEM((rows - 1, cols) + part, jnp.float32),
            pltpu.VMEM((cols,) + part, jnp.float32),
            pltpu.VMEM((cols - 1,) + part, jnp.float32),
            pltpu.SemaphoreType.DMA((4, 2, most)),
        ],
        compiler_params=pltpu.CompilerParams(collective_id=ident, has_side_effects=True),
    )(flat)


def half(ref, k, h, t):
    return ref[k, h, pl.ds(t, 1), :]


def walk(lines, tile, blocks, group, start, step):
    def outer(b, carry):
        def inner(j, carry):
            time = b * tile + j
            rising = b * (tile * lines) + j
            falling = (blocks - 1 - b) * (tile * lines) + (tile - 1 - j)
            tokens = [[base + line * tile for line in group] for base in (rising, falling)]
            return step(carry, tokens, time)

        return lax.fori_loop(0, tile, inner, carry, unroll=2)

    return lax.fori_loop(0, blocks, outer, start)


def groups_of(lines):
    size = 2 if lines % 2 == 0 else 1
    return [tuple(range(g, g + size)) for g in range(0, lines, size)]


def fold(ref, k, h, count):
    total = ref[k, h, pl.ds(0, count, stride=SUB), :]
    for s in range(1, SUB):
        total = total + ref[k, h, pl.ds(s, count, stride=SUB), :]
    return total


def softplus(x):
    return jnp.maximum(x, 0.0) + jnp.log1p(jnp.exp(-jnp.abs(x)))


def cross(a, b):
    return lax.dot_general(a, b, (((0,), (0,)), ((), ())), preferred_element_type=jnp.float32)


def back(a, b):
    return lax.dot_general(a, b, (((1,), (1,)), ((), ())), preferred_element_type=jnp.float32)


def block_kernel(
    tile_rows, tile_cols, states, rank,
    embedded_ref, upstream_ref, norm_gain_ref, in_weight_ref, scan_weight_ref, step_weight_ref,
    step_bias_ref, rate_ref, skip_ref, output_gain_ref, output_weight_ref,
    feature_ref, in_grad_ref, scan_grad_ref, stepw_ref, stepb_ref, dr_ref, skip_grad_ref,
    norm_grad_ref, gain_grad_ref, out_grad_ref,
    mixed, gate_grad, turn, along, down, wide, sv, steps, slope, low, hist, eight, pace8, up, dproj, sems,
):
    count, inner = tile_rows * tile_cols, output_weight_ref.shape[0]
    rows, cols = lax.axis_size("row"), lax.axis_size("col")
    eh, nh = inner // LANES, states // SUB
    group = rank + 2 * states
    shapes = ((tile_rows // cols, tile_cols), (tile_cols // rows, tile_rows))
    boxes = (along, down)
    axes = ("col", "row")
    greet(("row", "col"))

    def post(turn_number, pair):
        axis, box = axes[pair], boxes[pair]
        size = lax.axis_size(axis)
        me = lax.axis_index(axis)
        copies = []
        for d in range(1, size):
            target = lax.rem(me + d, size)
            copy = pltpu.make_async_remote_copy(
                src_ref=box.at[2 * turn_number, target],
                dst_ref=box.at[2 * turn_number + 1, me],
                send_sem=sems.at[turn_number, pair, 0, d],
                recv_sem=sems.at[turn_number, pair, 1, d],
                device_id={axis: target},
                device_id_type=MESH,
            )
            copy.start()
            copies.append(copy)
        box[2 * turn_number + 1, me] = box[2 * turn_number, me]
        return copies

    def finish(copies):
        for copy in copies:
            copy.wait()

    def put_home(turn_number, x):
        along[2 * turn_number] = x.reshape(along.shape[1:])
        first = post(turn_number, 0)
        for h in range(eh):
            turn[h] = x[:, h * LANES : (h + 1) * LANES]
        per = tile_cols // rows
        for c in range(tile_cols):
            for h in range(eh):
                down[
                    2 * turn_number, c // per,
                    (c % per) * tile_rows : (c % per + 1) * tile_rows,
                    h * LANES : (h + 1) * LANES,
                ] = turn[h, pl.ds(c, tile_rows, stride=tile_cols), :]
        return first, post(turn_number, 1)

    def take_home(turn_number):
        per = tile_cols // rows
        for c in range(tile_cols):
            for h in range(eh):
                turn[h, pl.ds(c, tile_rows, stride=tile_cols), :] = down[
                    2 * turn_number + 1, c // per,
                    (c % per) * tile_rows : (c % per + 1) * tile_rows,
                    h * LANES : (h + 1) * LANES,
                ]
        here = along[2 * turn_number + 1].reshape(count, inner)
        return here + jnp.concatenate([turn[h] for h in range(eh)], axis=1)

    def lines_in(turn_number, pair):
        return boxes[pair][2 * turn_number + 1].reshape(count, inner)

    def lines_out(turn_number, pair, x):
        boxes[pair][2 * turn_number] = x.reshape(boxes[pair].shape[1:])
        return post(turn_number, pair)

    def rate_of(d, m, h):
        return rate_ref[d, m * SUB : (m + 1) * SUB, h * LANES : (h + 1) * LANES]

    def part(h):
        return slice(h * LANES, (h + 1) * LANES)

    zero = jnp.zeros((SUB, LANES), jnp.float32)

    embedded = embedded_ref[...]
    normed = layer_norm(embedded, norm_gain_ref[...]).astype(jnp.bfloat16)
    mixed[...] = jnp.dot(normed, in_weight_ref[...], preferred_element_type=jnp.float32)
    values = jax.nn.silu(mixed[:, :inner]).astype(jnp.bfloat16).astype(jnp.float32)
    arriving = put_home(0, values)

    leaving = []
    for pair in range(2):
        lines, tile = shapes[pair]
        length = count // lines
        blocks = length // tile
        finish(arriving[pair])
        value = lines_in(0, pair)
        wide_p, sv_p, steps_p, hist_p = wide.at[pair], sv.at[pair], steps.at[pair], hist.at[pair]
        weight = scan_weight_ref[:, 2 * pair * group : 2 * (pair + 1) * group]
        projected = jnp.dot(
            value.astype(jnp.bfloat16), weight, preferred_element_type=jnp.float32
        )
        for k in range(2):
            d = 2 * pair + k
            lowrank = projected[:, k * group : k * group + rank]
            low[d] = lowrank
            before = (
                jnp.dot(
                    lowrank, step_weight_ref[d], precision=HIGHEST,
                    preferred_element_type=jnp.float32,
                )
                + step_bias_ref[d : d + 1, :]
            )
            slope[d] = jax.nn.sigmoid(before)
            pace = softplus(before)
            for h in range(eh):
                steps_p[k, h] = pace[:, part(h)]
                sv_p[k, h] = pace[:, part(h)] * value[:, part(h)]
            for which in range(2):
                for n in range(states):
                    col = k * group + rank + which * states + n
                    wide_p[k, which, pl.ds(n, count, stride=states), :] = jnp.broadcast_to(
                        projected[:, col : col + 1], (count, LANES)
                    )
            for h in range(eh):
                for line in range(lines):
                    at = line * (length + 1) * states
                    hist_p[k, h, at : at + states, :] = jnp.zeros((states, LANES), jnp.float32)
        for lot in groups_of(lines):

            def advance(carry, tokens, time):
                new = []
                i = 0
                for k in range(2):
                    for line, t in zip(lot, tokens[k]):
                        drive = [half(sv_p, k, h, t) for h in range(eh)]
                        pace = [half(steps_p, k, h, t) for h in range(eh)]
                        sums = [None] * eh
                        for m in range(nh):
                            at = pl.ds(pl.multiple_of(t * states + m * SUB, SUB), SUB)
                            slot = (line * (length + 1) + time + 1) * states + m * SUB
                            source = wide_p[k, 0, at, :]
                            probe = wide_p[k, 1, at, :]
                            for h in range(eh):
                                a = jnp.exp2(pace[h] * rate_of(2 * pair + k, m, h))
                                state = a * carry[i] + source * drive[h]
                                i += 1
                                hist_p[k, h, pl.ds(pl.multiple_of(slot, SUB), SUB), :] = state
                                new.append(state)
                                term = probe * state
                                sums[h] = term if sums[h] is None else sums[h] + term
                        for h in range(eh):
                            eight[k, h, pl.ds(pl.multiple_of(t * SUB, SUB), SUB), :] = sums[h]
                return tuple(new)

            walk(lines, tile, blocks, lot, (zero,) * (2 * len(lot) * eh * nh), advance)
        skip = skip_ref[2 * pair : 2 * pair + 1, :] + skip_ref[2 * pair + 1 : 2 * pair + 2, :]
        y = skip * value + jnp.concatenate(
            [fold(eight, 0, h, count) + fold(eight, 1, h, count) for h in range(eh)], axis=1
        )
        leaving.append(lines_out(1, pair, y))
    finish(leaving[0])
    finish(leaving[1])
    total = take_home(1)

    upstream = upstream_ref[...]
    gated, gate_pull = jax.vjp(gate_output, total, mixed[:, inner:], output_gain_ref[...])
    d_gated = back(upstream, output_weight_ref[...])
    d_total, d_gate_in, gain_grad = gate_pull(d_gated)
    arriving = put_home(2, d_total)
    gate_grad[...] = d_gate_in
    gain_grad_ref[...] = gain_grad
    out_grad_ref[...] = cross(gated.astype(jnp.bfloat16), upstream)

    leaving = []
    for pair in range(2):
        lines, tile = shapes[pair]
        length = count // lines
        blocks = length // tile
        finish(arriving[pair])
        g_all = lines_in(2, pair)
        wide_p, sv_p, steps_p, hist_p = wide.at[pair], sv.at[pair], steps.at[pair], hist.at[pair]
        for h in range(eh):
            up[0, h] = g_all[:, part(h)]
        for lot in groups_of(lines):

            def retreat(carry, tokens, time):
                grads, rates = carry
                rates = list(rates)
                new = []
                i = 0
                for k in range(2):
                    for line, t in zip(lot, tokens[1 - k]):
                        drive = [half(sv_p, k, h, t) for h in range(eh)]
                        pace = [half(steps_p, k, h, t) for h in range(eh)]
                        g = [half(up, 0, h, t) for h in range(eh)]
                        dd = [None] * eh
                        dp = [None] * eh
                        for m in range(nh):
                            at = pl.ds(pl.multiple_of(t * states + m * SUB, SUB), SUB)
                            slot = (line * (length + 1) + length - 1 - time) * states + m * SUB
                            earlier = pl.ds(pl.multiple_of(slot, SUB), SUB)
                            current = pl.ds(pl.multiple_of(slot + states, SUB), SUB)
                            source = wide_p[k, 0, at, :]
                            probe = wide_p[k, 1, at, :]
                            flow = None
                            read = None
                            for h in range(eh):
                                rate = rate_of(2 * pair + k, m, h)
                                grad = grads[i] + probe * g[h]
                                i += 1
                                term = grad * drive[h]
                                flow = term if flow is None else flow + term
                                term = g[h] * hist_p[k, h, current, :]
                                read = term if read is None else read + term
                                term = grad * source
                                dd[h] = term if dd[h] is None else dd[h] + term
                                carried = jnp.exp2(pace[h] * rate) * grad
                                q = carried * hist_p[k, h, earlier, :]
                                term = q * rate
                                dp[h] = term if dp[h] is None else dp[h] + term
                                j = (k * nh + m) * eh + h
                                rates[j] = rates[j] + q * pace[h]
                                new.append(carried)
                            wide_p[k, 0, at, :] = flow
                            wide_p[k, 1, at, :] = read
                        for h in range(eh):
                            at8 = pl.ds(pl.multiple_of(t * SUB, SUB), SUB)
                            eight[k, h, at8, :] = dd[h]
                            pace8[k, h, at8, :] = dp[h]
                return (tuple(new), tuple(rates))

            chains = 2 * len(lot) * eh * nh
            unused, rates = walk(
                lines, tile, blocks, lot, ((zero,) * chains, (zero,) * (2 * eh * nh)), retreat
            )
            for k in range(2):
                for m in range(nh):
                    for h in range(eh):
                        place = (2 * pair + k, slice(m * SUB, (m + 1) * SUB), part(h))
                        add = rates[(k * nh + m) * eh + h] * rate_ref[place] * (1.0 / LOG2E)
                        if lot[0] == 0:
                            dr_ref[place] = add
                        else:
                            dr_ref[place] += add
        value = lines_in(0, pair)
        g_all = lines_in(2, pair)
        skip = skip_ref[2 * pair : 2 * pair + 1, :] + skip_ref[2 * pair + 1 : 2 * pair + 2, :]
        dv = skip * g_all
        direct = jnp.sum(g_all * value, axis=0, keepdims=True)
        for k in range(2):
            d = 2 * pair + k
            skip_grad_ref[d : d + 1, :] = direct
            drive = jnp.concatenate([fold(eight, k, h, count) for h in range(eh)], axis=1)
            pace = jnp.concatenate([fold(pace8, k, h, count) for h in range(eh)], axis=1)
            dv = dv + drive * jnp.concatenate([steps_p[k, h] for h in range(eh)], axis=1)
            d_before = (drive * value + pace * (1.0 / LOG2E)) * slope[d]
            stepb_ref[d : d + 1, :] = jnp.sum(d_before, axis=0, keepdims=True)
            stepw_ref[d] = lax.dot_general(
                low[d], d_before, (((0,), (0,)), ((), ())), precision=HIGHEST,
                preferred_element_type=jnp.float32,
            )
            dproj[:, k * group : k * group + rank] = lax.dot_general(
                d_before, step_weight_ref[d], (((1,), (1,)), ((), ())), precision=HIGHEST,
                preferred_element_type=jnp.float32,
            )
            for which in range(2):
                for n in range(states):
                    col = k * group + rank + which * states + n
                    dproj[:, col : col + 1] = jnp.sum(
                        wide_p[k, which, pl.ds(n, count, stride=states), :], axis=-1, keepdims=True
                    )
        d_projected = dproj[...].astype(jnp.bfloat16)
        span = slice(2 * pair * group, 2 * (pair + 1) * group)
        leaving.append(lines_out(3, pair, back(d_projected, scan_weight_ref[:, span]) + dv))
        scan_grad_ref[:, span] = cross(value.astype(jnp.bfloat16), d_projected)
    finish(leaving[0])
    finish(leaving[1])
    d_values = take_home(3)

    d_mixed = jnp.concatenate(
        [d_values * silu_slope(mixed[:, :inner]), gate_grad[...]], axis=1
    ).astype(jnp.bfloat16)
    normed, norm_pull = jax.vjp(layer_norm, embedded_ref[...], norm_gain_ref[...])
    in_grad_ref[...] = cross(normed.astype(jnp.bfloat16), d_mixed)
    d_embedded, norm_grad_ref[...] = norm_pull(back(d_mixed, in_weight_ref[...]))
    feature_ref[...] = (upstream_ref[...].astype(jnp.float32) + d_embedded).astype(jnp.bfloat16)


def local(
    classes, features, cotangent, table, norm_gain, in_weight, scan_weight, step_weight,
    step_bias, decay_log, skip_gain, output_gain, output_weight,
):
    tile_rows, tile_cols, model_width = features.shape
    inner = output_weight.shape[0]
    count = tile_rows * tile_cols
    rows, cols = lax.axis_size("row"), lax.axis_size("col")
    rank = step_weight.shape[1]
    states = decay_log.shape[1]
    group = rank + 2 * states
    eh = inner // LANES
    lines = max(tile_rows // cols, tile_cols // rows)
    grad_scale = float(count * rows * cols) ** (-0.5)
    rate2 = -jnp.exp(decay_log) * LOG2E
    embedded = embed(features, classes, table).reshape(count, model_width)
    f32 = jnp.float32
    shapes = [
        ((count, model_width), jnp.bfloat16),
        (in_weight.shape, f32),
        (scan_weight.shape, f32),
        (step_weight.shape, f32),
        (step_bias.shape, f32),
        (decay_log.shape, f32),
        (skip_gain.shape, f32),
        ((1, model_width), f32),
        ((1, inner), f32),
        (output_weight.shape, f32),
    ]
    scratch = [
        ((count, 2 * inner), f32),
        ((count, inner), f32),
        ((eh, count, LANES), f32),
        ((8, cols, count // cols, inner), f32),
        ((8, rows, count // rows, inner), f32),
        ((2, 2, 2, count * states, LANES), f32),
        ((2, 2, eh, count, LANES), f32),
        ((2, 2, eh, count, LANES), f32),
        ((4, count, inner), f32),
        ((4, count, rank), f32),
        ((2, 2, eh, (count + lines) * states, LANES), f32),
        ((2, eh, count * SUB, LANES), f32),
        ((2, eh, count * SUB, LANES), f32),
        ((1, eh, count, LANES), f32),
        ((count, 2 * group), f32),
    ]
    feature_grad, *grads = pl.pallas_call(
        functools.partial(block_kernel, tile_rows, tile_cols, states, rank),
        out_shape=[jax.ShapeDtypeStruct(*s) for s in shapes],
        in_specs=[VMEM] * 11,
        out_specs=[VMEM] * 10,
        scratch_shapes=[pltpu.VMEM(*s) for s in scratch]
        + [pltpu.SemaphoreType.DMA((4, 2, 2, max(rows, cols)))],
        compiler_params=pltpu.CompilerParams(
            vmem_limit_bytes=BIG, collective_id=1, has_side_effects=True
        ),
    )(
        embedded, cotangent.reshape(count, model_width), norm_gain[None], in_weight, scan_weight,
        step_weight, step_bias, rate2, skip_gain, output_gain[None], output_weight,
    )
    feature_grad = feature_grad.reshape(tile_rows, tile_cols, model_width)
    grads[6], grads[7] = grads[6][0], grads[7][0]
    flat = jnp.concatenate([g.reshape(-1, LANES) for g in grads], axis=0)
    used = flat.shape[0]
    unit = rows * cols * SUB
    padded = -(-used // unit) * unit
    flat = jnp.pad(flat, ((0, padded - used), (0, 0))).reshape(rows, cols, padded // (rows * cols), LANES)
    flat = reduce_all(flat, 2).reshape(padded, LANES) * grad_scale
    summed = []
    place = 0
    for g in grads:
        length = g.size // LANES
        summed.append(flat[place : place + length].reshape(g.shape))
        place += length
    return (feature_grad, *summed)


def solution(mesh):
    in_specs = (P("row", "col"), P("row", "col", None), P("row", "col", None)) + (P(),) * 10
    out_specs = (P("row", "col", None),) + (P(),) * 9
    return jax.shard_map(local, mesh=mesh, in_specs=in_specs, out_specs=out_specs, check_vma=False)
```

time: 186 us -> 117 us (0.63)
  Pallas kernels: 132 us -> 99.3 us
  local copies, waits for them, and re-layouts: 27.4 us -> 13 us
  other arithmetic: 13.1 us -> 2.73 us
  matrix products: 10.9 us -> 0.92 us
    pallas_call x8 -> x1, Pallas kernels: 97.9 us -> 65.5 us  [local(): pl.pallas_call(functools.partial(block_kernel, tile_rows, tile_cols, stat...]
    dot_general x23 -> x0, matrix products: 9.67 us -> none  [the longest x4 1.77 us: local(): jnp.dot(lowrank[i], step_weight[dirs[i]], precision=HIGHEST)]
    unnamed x77 -> x23, local copies, waits for them, and re-layouts: 12.2 us -> 3.11 us
    reshape x6, local copies, waits for them, and re-layouts: 0.27 us -> 3.38 us  [local(): flat = jnp.concatenate([g.reshape(-1, LANES) for g in grads], axis=0)]
    slice x7 -> x0, local copies, waits for them, and re-layouts: 2.67 us -> none  [the longest x2 1.44 us: local(): parts.append(dflow[:, i * 2 * states:(i + 1) * 2 * states])]
    transpose x2 -> x0, local copies, waits for them, and re-layouts: 2.3 us -> none  [from_lines(): d = jnp.swapaxes(d.reshape(tile_cols, tile_rows, d.shape[-1]), 0, 1)]
    select_n x2 -> x0, other arithmetic: 2.14 us -> none  [local(): steps = jax.nn.softplus(before)]
    another operation x6 -> x0, other arithmetic: 2.1 us -> none
where the time goes in v1:
time: 117 us
  Pallas kernels  99.3 us (85%)
  local copies, waits for them, and re-layouts  13 us (11%)
  other arithmetic  2.73 us (2%)
    pallas_call x1, Pallas kernels, local(): pl.pallas_call(functools.partial(block_kernel, tile_rows, tile_cols, stat...  65.5 us
    pallas_call x1, Pallas kernels, reduce_all(): pl.pallas_call(reduce_kernel, out_shape=jax.ShapeDtypeStruct(flat.shape,...  33.8 us
    reshape x8, local copies, waits for them, and re-layouts, local(): summed.append(flat[place:place + length].reshape(g.shape))  4.43 us
    reshape x6, local copies, waits for them, and re-layouts, local(): flat = jnp.concatenate([g.reshape(-1, LANES) for g in grads], axis=0)  3.38 us
    unnamed x23, local copies, waits for them, and re-layouts  3.11 us

profile of v1, /device:TPU:1, one launch (start us, length us, event | category | flops | bytes accessed | tf_op | source)
XLA Modules:
  0.0 116.8 jit_solution(13892013931264298542)
XLA Ops:
  0.6 0.0 copy-start
  0.7 0.0 copy-start.4
  0.7 0.0 copy-start.7
  0.7 1.5 %negate_multiply_fusion.rate_ref = f32[4,16,256]{2,1,0:T(8,128)} fusion(f32[4,16,256]{2,1,0:T(8,128)} %param.22), kind=kLoop, calls=%fused_computation.3 | loop fusion | flops 32768 | bytes 131072 | tf_op jit(solution)/shard_map/mul | solution.py:459
  2.2 0.0 copy-done
  2.2 0.0 copy-done.4
  2.2 0.0 copy-done.7
  2.2 0.0 copy-start.3
  2.2 0.9 convolution_add_fusion
  3.1 0.0 copy-done.3
  3.1 0.8 copy.24.scan_weight_ref
  3.9 65.5 %shard_map.204 = (bf16[256,128]{1,0:T(8,128)(2,1)}, f32[128,512]{1,0:T(8,128)}, f32[256,160]{1,0:T(8,128)}, f32[4,8,256]{2,1,0:T(8,128)}, f32[4,256]{1,0:T(4,128...) custom-call(f32[256,128]{1,0:T(8,128)} %bitcast.24, ...), custom_call_target="tpu_custom_call" | custom-call | tf_op jit(solution)/shard_map/pallas_call | solution.py:491
  69.4 0.0 copy-start.6
  69.4 0.7 reshape.84
  70.2 0.7 reshape.86
  70.8 0.8 reshape.83
  71.6 0.0 copy-done.6
  71.6 0.0 copy-start.1
  71.6 1.2 %reshape.82 = f32[320,128]{1,0:T(8,128)S(1)} reshape(f32[256,160]{1,0:T(8,128)} %get-tuple-element.22) | data formatting | bytes 327680 | tf_op jit(solution)/shard_map/reshape | solution.py:507
  72.8 0.0 copy-done.1
  72.8 0.0 copy-start.2
  72.8 0.0 copy-start.8
  72.8 0.0 copy-start.9
  72.9 0.8 copy-done.2
  73.7 0.0 copy-done.8
  73.7 0.0 copy-done.9
  73.7 0.4 concatenate.3
  74.2 0.9 pad.4
  75.1 33.8 %shard_map.205 = f32[8,4,48,128]{3,2,1,0:T(8,128)} custom-call(f32[8,4,48,128]{3,2,1,0:T(8,128)} %bitcast.15), custom_call_target="tpu_custom_call" | custom-call | tf_op jit(solution)/shard_map/pallas_call | solution.py:100
  108.9 1.2 %broadcast_multiply_fusion = f32[8,4,48,128]{3,2,1,0:T(8,128)S(1)} fusion(f32[8,4,48,128]{3,2,1,0:T(8,128)} %shard_map.205), kind=kLoop, calls=%fused_computation.1 | loop fusion | flops 196608 | bytes 1572864 | tf_op jit(solution)/shard_map/mul | solution.py:512
  110.2 0.5 slice_bitcast_fusion.1
  110.7 0.6 slice_bitcast_fusion
  111.2 0.6 reshape.93
  111.8 0.6 reshape.91
  112.5 0.6 reshape.90
  113.1 0.6 reshape.92
  113.7 0.7 slice.44
  114.4 0.7 reshape.88
  115.2 0.1 reshape.89
  115.3 0.0 copy-start.5
  115.3 0.8 copy.25
  116.1 0.1 copy-done.5
  116.2 0.6 copy.27
  (7 shorter events, 0.1 us)
Async XLA Ops:
  0.6 1.6 %copy-start = (f32[16,128]{1,0:T(8,128)S(1)}, f32[16,128]{1,0:T(8,128)}, u32[]{:S(2)}) copy-start(f32[16,128]{1,0:T(8,128)} %param.16) | copy-start | bytes 24580
  0.7 1.5 %copy-start.4 = (bf16[16,16,128]{2,1,0:T(8,128)(2,1)S(1)}, bf16[16,16,128]{2,1,0:T(8,128)(2,1)}, u32[]{:S(2)}) copy-start(bf16[16,16,128]{2,1,0:T(8,128)(2,1)} %param.14) | copy-start | bytes 196612
  0.7 1.5 %copy-start.7 = (s32[16,16]{1,0:T(8,128)S(1)}, s32[16,16]{1,0:T(8,128)}, u32[]{:S(2)}) copy-start(s32[16,16]{1,0:T(8,128)} %param.13) | copy-start | bytes 3076
  2.2 0.9 copy-start.3
  69.4 2.2 %copy-start.6 = (f32[4,16,256]{2,1,0:T(8,128)S(1)}, f32[4,16,256]{2,1,0:T(8,128)}, u32[]{:S(2)}) copy-start(f32[4,16,256]{2,1,0:T(8,128)} %get-tuple-element.25) | copy-start | bytes 196612
  71.6 1.2 %copy-start.1 = (f32[128,512]{1,0:T(8,128)S(1)}, f32[128,512]{1,0:T(8,128)}, u32[]{:S(2)}) copy-start(f32[128,512]{1,0:T(8,128)} %get-tuple-element.21) | copy-start | bytes 786436
  72.8 0.9 copy-start.2
  72.8 0.9 copy-start.8
  72.8 0.9 copy-start.9
  115.3 0.8 copy-start.5

commit v2 on v1

--- a/solution.py
+++ b/solution.py
@@ -55,63 +55,6 @@
     pl.semaphore_wait(barrier, partners)
 
 
-def reduce_kernel(x_ref, out_ref, first, partial, second, sems):
-    rows, cols = lax.axis_size("row"), lax.axis_size("col")
-    r, c = lax.axis_index("row"), lax.axis_index("col")
-    greet(("row", "col"))
-
-    def spread(axis, source, result, phase):
-        count = lax.axis_size(axis)
-        me = lax.axis_index(axis)
-        copies = []
-        for d in range(1, count):
-            target = lax.rem(me + d, count)
-            copy = pltpu.make_async_remote_copy(
-                src_ref=source(target),
-                dst_ref=result(me, d),
-                send_sem=sems.at[phase, 0, d],
-                recv_sem=sems.at[phase, 1, d],
-                device_id={axis: target},
-                device_id_type=MESH,
-            )
-            copy.start()
-            copies.append(copy)
-        for copy in copies:
-            copy.wait()
-
-    spread("row", lambda t: x_ref.at[t], lambda me, d: first.at[d - 1], 0)
-    acc = x_ref[r]
-    for d in range(rows - 1):
-        acc = acc + first[d]
-    partial[...] = acc
-    spread("col", lambda t: partial.at[t], lambda me, d: second.at[d - 1], 1)
-    acc = partial[c]
-    for d in range(cols - 1):
-        acc = acc + second[d]
-    out_ref[r, c] = acc
-    spread("col", lambda t: out_ref.at[r, c], lambda me, d: out_ref.at[r, me], 2)
-    spread("row", lambda t: out_ref.at[r], lambda me, d: out_ref.at[me], 3)
-
-
-def reduce_all(flat, ident):
-    rows, cols = lax.axis_size("row"), lax.axis_size("col")
-    part = flat.shape[2:]
-    most = max(rows, cols)
-    return pl.pallas_call(
-        reduce_kernel,
-        out_shape=jax.ShapeDtypeStruct(flat.shape, flat.dtype),
-        in_specs=[VMEM],
-        out_specs=VMEM,
-        scratch_shapes=[
-            pltpu.VMEM((rows - 1, cols) + part, jnp.float32),
-            pltpu.VMEM((cols,) + part, jnp.float32),
-            pltpu.VMEM((cols - 1,) + part, jnp.float32),
-            pltpu.SemaphoreType.DMA((4, 2, most)),
-        ],
-        compiler_params=pltpu.CompilerParams(collective_id=ident, has_side_effects=True),
-    )(flat)
-
-
 def half(ref, k, h, t):
     return ref[k, h, pl.ds(t, 1), :]
 
@@ -155,12 +98,13 @@
 
 
 def block_kernel(
-    tile_rows, tile_cols, states, rank,
+    tile_rows, tile_cols, states, rank, grad_scale, tiles,
     embedded_ref, upstream_ref, norm_gain_ref, in_weight_ref, scan_weight_ref, step_weight_ref,
     step_bias_ref, rate_ref, skip_ref, output_gain_ref, output_weight_ref,
     feature_ref, in_grad_ref, scan_grad_ref, stepw_ref, stepb_ref, dr_ref, skip_grad_ref,
     norm_grad_ref, gain_grad_ref, out_grad_ref,
-    mixed, gate_grad, turn, along, down, wide, sv, steps, slope, low, hist, eight, pace8, up, dproj, sems,
+    mixed, gate_grad, turn, along, down, wide, sv, steps, slope, low, hist, eight, pace8, up, dproj, dr_acc,
+    mine0, from0, side0, all0, mine1, from1, side1, all1, sems, sumsems,
 ):
     count, inner = tile_rows * tile_cols, output_weight_ref.shape[0]
     rows, cols = lax.axis_size("row"), lax.axis_size("col")
@@ -236,6 +180,89 @@
         return slice(h * LANES, (h + 1) * LANES)
 
     zero = jnp.zeros((SUB, LANES), jnp.float32)
+
+    sums = ((mine0, from0, side0, all0), (mine1, from1, side1, all1))
+    fill = [0, 0]
+
+    def put(lot, x):
+        mine = sums[lot][0]
+        per = mine.shape[1] // SUB
+        for i in range(x.shape[0] // SUB):
+            tile = fill[lot]
+            at = (tile % per) * SUB
+            mine[tile // per, at : at + SUB, :] = x[i * SUB : (i + 1) * SUB]
+            fill[lot] += 1
+
+    def put_wide(lot, x):
+        for h in range(x.shape[1] // LANES):
+            put(lot, x[:, h * LANES : (h + 1) * LANES])
+
+    taken = [0, 0]
+
+    def take(lot, height):
+        full = sums[lot][3]
+        per = full.shape[1] // SUB
+        out = []
+        for i in range(height // SUB):
+            tile = taken[lot]
+            at = (tile % per) * SUB
+            out.append(full[tile // per, at : at + SUB, :])
+            taken[lot] += 1
+        return jnp.concatenate(out, axis=0) * grad_scale
+
+    def take_wide(lot, height, width):
+        return jnp.concatenate([take(lot, height) for h in range(width // LANES)], axis=1)
+
+    def pad_rows(*rows_in):
+        missing = -len(rows_in) % SUB
+        return jnp.concatenate(list(rows_in) + [jnp.zeros((missing, LANES), jnp.float32)], axis=0)
+
+    def pad_lot(lot):
+        while fill[lot] < tiles[lot]:
+            put(lot, zero)
+
+    def spread(lot, phase, axis, source, result):
+        size = lax.axis_size(axis)
+        me = lax.axis_index(axis)
+        copies = []
+        for d in range(1, size):
+            target = lax.rem(me + d, size)
+            copy = pltpu.make_async_remote_copy(
+                src_ref=source(target),
+                dst_ref=result(me, d),
+                send_sem=sumsems.at[lot, phase, 0, d],
+                recv_sem=sumsems.at[lot, phase, 1, d],
+                device_id={axis: target},
+                device_id_type=MESH,
+            )
+            copy.start()
+            copies.append(copy)
+        return copies
+
+    def sum_scatter(lot):
+        mine, other, side, full = sums[lot]
+        pad_lot(lot)
+        return spread(lot, 0, "row", lambda t: mine.at[t], lambda me, d: other.at[d - 1])
+
+    def sum_across(lot, copies):
+        mine, other, side, full = sums[lot]
+        finish(copies)
+        acc = mine[lax.axis_index("row")]
+        for d in range(rows - 1):
+            acc = acc + other[d]
+        me = lax.axis_index("col")
+        side[me] = acc
+        return spread(lot, 1, "col", lambda t: side.at[me], lambda m, d: side.at[m])
+
+    def sum_gather(lot, copies):
+        mine, other, side, full = sums[lot]
+        finish(copies)
+        acc = side[0]
+        for d in range(1, cols):
+            acc = acc + side[d]
+        me = lax.axis_index("row")
+        full[me] = acc
+        return spread(lot, 2, "row", lambda t: full.at[me], lambda m, d: full.at[m])
 
     embedded = embedded_ref[...]
     normed = layer_norm(embedded, norm_gain_ref[...]).astype(jnp.bfloat16)
@@ -324,8 +351,8 @@
     d_total, d_gate_in, gain_grad = gate_pull(d_gated)
     arriving = put_home(2, d_total)
     gate_grad[...] = d_gate_in
-    gain_grad_ref[...] = gain_grad
-    out_grad_ref[...] = cross(gated.astype(jnp.bfloat16), upstream)
+    put(0, pad_rows(*[gain_grad[:, part(h)] for h in range(eh)]))
+    put_wide(0, cross(gated.astype(jnp.bfloat16), upstream))
 
     leaving = []
     for pair in range(2):
@@ -395,51 +422,92 @@
                         place = (2 * pair + k, slice(m * SUB, (m + 1) * SUB), part(h))
                         add = rates[(k * nh + m) * eh + h] * rate_ref[place] * (1.0 / LOG2E)
                         if lot[0] == 0:
-                            dr_ref[place] = add
+                            dr_acc[place] = add
                         else:
-                            dr_ref[place] += add
+                            dr_acc[place] += add
         value = lines_in(0, pair)
         g_all = lines_in(2, pair)
         skip = skip_ref[2 * pair : 2 * pair + 1, :] + skip_ref[2 * pair + 1 : 2 * pair + 2, :]
         dv = skip * g_all
         direct = jnp.sum(g_all * value, axis=0, keepdims=True)
+        small = [direct[:, part(h)] for h in range(eh)]
         for k in range(2):
             d = 2 * pair + k
-            skip_grad_ref[d : d + 1, :] = direct
             drive = jnp.concatenate([fold(eight, k, h, count) for h in range(eh)], axis=1)
             pace = jnp.concatenate([fold(pace8, k, h, count) for h in range(eh)], axis=1)
             dv = dv + drive * jnp.concatenate([steps_p[k, h] for h in range(eh)], axis=1)
             d_before = (drive * value + pace * (1.0 / LOG2E)) * slope[d]
-            stepb_ref[d : d + 1, :] = jnp.sum(d_before, axis=0, keepdims=True)
-            stepw_ref[d] = lax.dot_general(
-                low[d], d_before, (((0,), (0,)), ((), ())), precision=HIGHEST,
-                preferred_element_type=jnp.float32,
-            )
+            bias_sum = jnp.sum(d_before, axis=0, keepdims=True)
+            small += [bias_sum[:, part(h)] for h in range(eh)]
+            put_wide(
+                pair,
+                lax.dot_general(
+                    low[d], d_before, (((0,), (0,)), ((), ())), precision=HIGHEST,
+                    preferred_element_type=jnp.float32,
+                ),
+            )
+            put_wide(pair, dr_acc[d])
             dproj[:, k * group : k * group + rank] = lax.dot_general(
                 d_before, step_weight_ref[d], (((1,), (1,)), ((), ())), precision=HIGHEST,
                 preferred_element_type=jnp.float32,
             )
-            for which in range(2):
-                for n in range(states):
-                    col = k * group + rank + which * states + n
-                    dproj[:, col : col + 1] = jnp.sum(
-                        wide_p[k, which, pl.ds(n, count, stride=states), :], axis=-1, keepdims=True
-                    )
+            lane = lax.broadcasted_iota(jnp.int32, (LANES, 2 * states), 1)
+            flow = None
+            for j in range(2 * states):
+                x = wide_p[k, j // states, pl.ds(j % states, count, stride=states), :]
+                pick = (lane == j).astype(jnp.bfloat16)
+                term = jnp.dot(x.astype(jnp.bfloat16), pick, preferred_element_type=jnp.float32)
+                flow = term if flow is None else flow + term
+            dproj[:, k * group + rank : (k + 1) * group] = flow
         d_projected = dproj[...].astype(jnp.bfloat16)
         span = slice(2 * pair * group, 2 * (pair + 1) * group)
         leaving.append(lines_out(3, pair, back(d_projected, scan_weight_ref[:, span]) + dv))
-        scan_grad_ref[:, span] = cross(value.astype(jnp.bfloat16), d_projected)
+        put(pair, pad_rows(*small))
+        put_wide(pair, cross(d_projected, value.astype(jnp.bfloat16)))
+        if pair == 0:
+            early = sum_scatter(0)
+        else:
+            early = sum_across(0, early)
     finish(leaving[0])
     finish(leaving[1])
     d_values = take_home(3)
+    early = sum_gather(0, early)
 
     d_mixed = jnp.concatenate(
         [d_values * silu_slope(mixed[:, :inner]), gate_grad[...]], axis=1
     ).astype(jnp.bfloat16)
     normed, norm_pull = jax.vjp(layer_norm, embedded_ref[...], norm_gain_ref[...])
-    in_grad_ref[...] = cross(normed.astype(jnp.bfloat16), d_mixed)
-    d_embedded, norm_grad_ref[...] = norm_pull(back(d_mixed, in_weight_ref[...]))
+    put_wide(1, cross(normed.astype(jnp.bfloat16), d_mixed))
+    d_embedded, norm_grad = norm_pull(back(d_mixed, in_weight_ref[...]))
+    put(1, pad_rows(norm_grad))
+    late = sum_scatter(1)
     feature_ref[...] = (upstream_ref[...].astype(jnp.float32) + d_embedded).astype(jnp.bfloat16)
+    late = sum_across(1, late)
+    finish(early)
+    late = sum_gather(1, late)
+
+    def take_pair(pair):
+        for d in (2 * pair, 2 * pair + 1):
+            stepw_ref[d] = take_wide(pair, rank, inner)
+            dr_ref[d] = take_wide(pair, states, inner)
+        small = take(pair, -(-3 * eh // SUB) * SUB)
+        for h in range(eh):
+            for k in range(2):
+                d = 2 * pair + k
+                skip_grad_ref[d : d + 1, part(h)] = small[h : h + 1]
+                stepb_ref[d : d + 1, part(h)] = small[(k + 1) * eh + h : (k + 1) * eh + h + 1]
+        span = slice(2 * pair * group, 2 * (pair + 1) * group)
+        scan_grad_ref[:, span] = take_wide(pair, 2 * group, inner).T
+
+    small = take(0, SUB)
+    for h in range(eh):
+        gain_grad_ref[:, part(h)] = small[h : h + 1]
+    out_grad_ref[...] = take_wide(0, inner, out_grad_ref.shape[1])
+    take_pair(0)
+    finish(late)
+    take_pair(1)
+    in_grad_ref[...] = take_wide(1, in_grad_ref.shape[0], in_grad_ref.shape[1])
+    norm_grad_ref[...] = take(1, SUB)[0:1]
 
 
 def local(
@@ -487,14 +555,27 @@
         ((2, eh, count * SUB, LANES), f32),
         ((1, eh, count, LANES), f32),
         ((count, 2 * group), f32),
+        (decay_log.shape, f32),
     ]
+    pair_tiles = eh * (2 * rank + 2 * states + 2 * group) // SUB + -(-3 * eh // SUB)
+    least = (
+        1 + inner * model_width // (LANES * SUB) + pair_tiles,
+        1 + in_weight.size // (LANES * SUB) + pair_tiles,
+    )
+    tiles = tuple(-(-t // rows) * rows for t in least)
+    for lot in range(2):
+        chunk = (tiles[lot] // rows * SUB, LANES)
+        scratch += [((rows,) + chunk, f32), ((rows - 1,) + chunk, f32), ((cols,) + chunk, f32), ((rows,) + chunk, f32)]
     feature_grad, *grads = pl.pallas_call(
-        functools.partial(block_kernel, tile_rows, tile_cols, states, rank),
+        functools.partial(block_kernel, tile_rows, tile_cols, states, rank, grad_scale, tiles),
         out_shape=[jax.ShapeDtypeStruct(*s) for s in shapes],
         in_specs=[VMEM] * 11,
         out_specs=[VMEM] * 10,
         scratch_shapes=[pltpu.VMEM(*s) for s in scratch]
-        + [pltpu.SemaphoreType.DMA((4, 2, 2, max(rows, cols)))],
+        + [
+            pltpu.SemaphoreType.DMA((4, 2, 2, max(rows, cols))),
+            pltpu.SemaphoreType.DMA((2, 3, 2, max(rows, cols))),
+        ],
         compiler_params=pltpu.CompilerParams(
             vmem_limit_bytes=BIG, collective_id=1, has_side_effects=True
         ),
@@ -504,19 +585,7 @@
     )
     feature_grad = feature_grad.reshape(tile_rows, tile_cols, model_width)
     grads[6], grads[7] = grads[6][0], grads[7][0]
-    flat = jnp.concatenate([g.reshape(-1, LANES) for g in grads], axis=0)
-    used = flat.shape[0]
-    unit = rows * cols * SUB
-    padded = -(-used // unit) * unit
-    flat = jnp.pad(flat, ((0, padded - used), (0, 0))).reshape(rows, cols, padded // (rows * cols), LANES)
-    flat = reduce_all(flat, 2).reshape(padded, LANES) * grad_scale
-    summed = []
-    place = 0
-    for g in grads:
-        length = g.size // LANES
-        summed.append(flat[place : place + length].reshape(g.shape))
-        place += length
-    return (feature_grad, *summed)
+    return (feature_grad, *grads)
 
 
 def solution(mesh):

time: 117 us -> 99.6 us (0.85)
  Pallas kernels: 99.3 us -> 87.7 us
  local copies, waits for them, and re-layouts: 13 us -> 8.37 us
  other arithmetic: 2.73 us -> 1.52 us
    pallas_call x1 -> x0, Pallas kernels: 33.8 us -> none  [reduce_all(): pl.pallas_call(reduce_kernel, out_shape=jax.ShapeDtypeStruct(flat.shape,...]
    pallas_call x1, Pallas kernels: 65.5 us -> 87.7 us  [local(): pl.pallas_call(functools.partial(block_kernel, tile_rows, tile_cols, stat...]
    reshape x14 -> x0, local copies, waits for them, and re-layouts: 7.8 us -> none  [the longest x8 4.43 us: local(): summed.append(flat[place:place + length].reshape(g.shape))]
    unnamed x23 -> x37, local copies, waits for them, and re-layouts: 3.11 us -> 8.37 us
    mul x1 -> x0, other arithmetic: 1.21 us -> none  [local(): flat = reduce_all(flat, 2).reshape(padded, LANES) * grad_scale]
where the time goes in v2:
time: 99.6 us; the launch traced here: 99.2 us
  Pallas kernels  87.7 us (88%)
  local copies, waits for them, and re-layouts  8.37 us (8%)
  other arithmetic  1.52 us (2%)
    pallas_call x1, Pallas kernels, local(): pl.pallas_call(functools.partial(block_kernel, tile_rows, tile_cols, stat...  87.7 us
    unnamed x37, local copies, waits for them, and re-layouts  8.37 us

profile of v2, /device:TPU:1, one launch (start us, length us, event | category | flops | bytes accessed | tf_op | source)
XLA Modules:
  0.0 99.2 jit_solution(17494533834338341345)
XLA Ops:
  0.6 0.0 copy-start
  0.7 0.0 copy-start.4
  0.7 0.0 copy-start.8
  0.7 1.5 %negate_multiply_fusion.rate_ref = f32[4,16,256]{2,1,0:T(8,128)} fusion(f32[4,16,256]{2,1,0:T(8,128)} %param.22), kind=kLoop, calls=%fused_computation.2 | loop fusion | flops 32768 | bytes 131072 | tf_op jit(solution)/shard_map/mul | solution.py:527
  2.2 0.0 copy-done
  2.2 0.0 copy-done.4
  2.2 0.0 copy-done.8
  2.2 0.0 copy-start.3
  2.2 0.9 convolution_add_fusion
  3.1 0.0 copy-done.3
  3.1 0.8 copy.23.scan_weight_ref
  3.9 87.7 %shard_map.204 = (bf16[256,128]{1,0:T(8,128)(2,1)}, f32[128,512]{1,0:T(8,128)}, f32[256,160]{1,0:T(8,128)}, f32[4,8,256]{2,1,0:T(8,128)}, f32[4,256]{1,0:T(4,128...) custom-call(f32[256,128]{1,0:T(8,128)} %bitcast.10, ...), custom_call_target="tpu_custom_call" | custom-call | tf_op jit(solution)/shard_map/pallas_call | solution.py:569
  91.6 0.0 copy-start.6
  91.6 0.0 copy-start.1
  91.6 1.8 %copy.24 = f32[256,160]{0,1:T(8,128)} copy(f32[256,160]{1,0:T(8,128)} %get-tuple-element.32) | data formatting | bytes 327680
  93.4 0.0 copy-done.6
  93.4 0.6 copy.34
  94.0 0.0 copy-done.1
  94.0 0.0 copy-start.7
  94.0 0.0 copy-start.10
  94.0 0.0 copy-start.5
  94.0 0.7 copy.35
  94.7 0.0 copy-done.7
  94.7 0.0 copy-start.2
  94.7 0.6 copy.36
  95.4 0.0 copy-done.10
  95.4 0.6 copy.37
  96.0 0.0 copy-done.5
  96.0 0.0 copy-start.9
  96.0 0.6 copy.38
  96.6 0.0 copy-done.9
  96.6 0.0 copy-start.12
  96.6 0.6 copy.39
  97.2 0.1 copy-done.12
  97.3 0.0 copy-start.11
  97.3 0.5 copy.40
  97.8 0.1 copy-done.11
  98.0 0.6 copy.41
  98.5 0.0 copy-done.2
  98.5 0.7 copy.42
Async XLA Ops:
  0.6 1.6 %copy-start = (f32[16,128]{1,0:T(8,128)S(1)}, f32[16,128]{1,0:T(8,128)}, u32[]{:S(2)}) copy-start(f32[16,128]{1,0:T(8,128)} %param.16) | copy-start | bytes 24580
  0.7 1.5 %copy-start.4 = (bf16[16,16,128]{2,1,0:T(8,128)(2,1)S(1)}, bf16[16,16,128]{2,1,0:T(8,128)(2,1)}, u32[]{:S(2)}) copy-start(bf16[16,16,128]{2,1,0:T(8,128)(2,1)} %param.14) | copy-start | bytes 196612
  0.7 1.5 %copy-start.8 = (s32[16,16]{1,0:T(8,128)S(1)}, s32[16,16]{1,0:T(8,128)}, u32[]{:S(2)}) copy-start(s32[16,16]{1,0:T(8,128)} %param.13) | copy-start | bytes 3076
  2.2 0.9 copy-start.3
  91.6 1.8 %copy-start.6 = (bf16[256,128]{1,0:T(8,128)(2,1)S(1)}, bf16[256,128]{1,0:T(8,128)(2,1)}, u32[]{:S(2)}) copy-start(bf16[256,128]{1,0:T(8,128)(2,1)} %get-tuple-element.20) | copy-start | bytes 196612
  91.6 2.4 %copy-start.1 = (f32[128,512]{1,0:T(8,128)S(1)}, f32[128,512]{1,0:T(8,128)}, u32[]{:S(2)}) copy-start(f32[128,512]{1,0:T(8,128)} %get-tuple-element.51) | copy-start | bytes 786436
  94.0 0.8 copy-start.7
  94.0 1.4 %copy-start.10 = (f32[4,256]{1,0:T(4,128)S(1)}, f32[4,256]{1,0:T(4,128)}, u32[]{:S(2)}) copy-start(f32[4,256]{1,0:T(4,128)} %get-tuple-element.54) | copy-start | bytes 12292
  94.0 2.0 %copy-start.5 = (f32[4,16,256]{2,1,0:T(8,128)S(1)}, f32[4,16,256]{2,1,0:T(8,128)}, u32[]{:S(2)}) copy-start(f32[4,16,256]{2,1,0:T(8,128)} %get-tuple-element.55) | copy-start | bytes 196612
  94.7 3.8 %copy-start.2 = (f32[256,128]{1,0:T(8,128)S(1)}, f32[256,128]{1,0:T(8,128)}, u32[]{:S(2)}) copy-start(f32[256,128]{1,0:T(8,128)} %get-tuple-element.59) | copy-start | bytes 393220
  96.0 0.7 copy-start.9
  96.6 0.7 copy-start.12
  97.3 0.7 copy-start.11
